TPU v7x, 256 devices: a whole 4x4x8 slice. The times are simulated.
256 devices in a mesh: member: 4 (over y_hi, core), node: 64 (over y_lo, x, z).
Axes of the slice: x: 4, y: 4 (y_hi: 2, y_lo: 2; y = y_hi * 2 + y_lo), z: 8, core: 2. Of those that a mesh axis runs over, the one named last changes fastest.
Arguments:
- gridpoint_state: bfloat16 [218, 65536], P(None, 'node'), may hold values from -6 to 6
- grid_truth: bfloat16 [100, 65536], P(None, 'node'), may hold values from -6 to 6
- encoder_slots: int32 [16384, 16], P('node'), may hold values from 0 to 65535, as said below
- encoder_count: int32 [16384], P('node'), may hold values from 1 to 16
- node_reach: int32 [16384], P('node'), may hold values from 128 to 256
- decoder_slots: int32 [65536, 4], P('node'), may hold values from 0 to 16383, as said below
- member_perturb: bfloat16 [4, 16384, 1024], P('member', 'node'), may hold values from -6 to 6
- embed_weight: bfloat16 [218, 1024], replicated, may hold values from -0.4375 to 0.4375
- norm_gains: float32 [3, 1024], replicated, may hold values from 0.1 to 1.9
- qkv_weight: bfloat16 [1024, 3072], replicated
- out_weight: bfloat16 [1024, 1024], replicated, may hold values from -0.1875 to 0.1875
- up_weight: bfloat16 [1024, 4096], P('node'), may hold values from -0.1875 to 0.1875
- down_weight: bfloat16 [1024, 4096], P('node'), may hold values from -0.09375 to 0.09375
- head_weight: bfloat16 [1024, 100], replicated, may hold values from -0.1875 to 0.1875
Outputs:
- crps_grad: float32 [4, 100, 65536], P('member', None, 'node')
Inputs may be any that keep to these rules, and one draw needn't show every extreme that they name: `encoder_slots`: for a hidden node of region r (nodes r * 256 to (r + 1) * 256 - 1), every slot names a grid point of region r - 1, r or r + 1, a region holding 1024 consecutive points; slots from encoder_count on are padding. `decoder_slots`: for a grid point of region r, every slot names a hidden node of region r - 1, r or r + 1.
All inputs are finite; a program needn't handle non-finite values.
Results may differ from a plain program's by a relative error of at most 0.0095.
The roundings to bfloat16 on the way count: a program that leaves them out, or rounds other values in their place, can miss the bound.
Values may be sent and summed in bfloat16 or wider, within the bound.
No kernel may reach another device: no remote copies, remote signals or barrier semaphores. Data moves between devices by JAX's collectives and lax.ppermute only.
A program may use at most 128 MiB of HBM per device.

v0:
```python
import jax
import jax.numpy as jnp
from jax import lax
from jax.sharding import Mesh
from jax.sharding import PartitionSpec as P

HEADS = 16
HEAD_DIM = 64
BAND = 256
NODE = ("node_0", "node_1", "node_2")
EPS = 1e-05
SMOOTH = 0.25


def with_halo(block, sides, width):
    for axis, dim in sides:
        count = lax.axis_size(axis)
        forward = [(i, i + 1) for i in range(count - 1)]
        backward = [(target, source) for source, target in forward]
        low = lax.ppermute(
            lax.slice_in_dim(block, block.shape[dim] - width, None, axis=dim), axis, forward
        )
        high = lax.ppermute(lax.slice_in_dim(block, 0, width, axis=dim), axis, backward)
        block = jnp.concatenate([low, block, high], axis=dim)
    return block


def in_order(blocks, dim):
    blocks = jnp.moveaxis(blocks, 0, dim)
    dims = blocks.shape
    return blocks.reshape(*dims[:dim], dims[dim] * dims[dim + 1], *dims[dim + 2 :])


def gather_in_order(shard, axes, sequence):
    blocks = shard[None]
    for k in sequence:
        blocks = lax.all_gather(blocks, axes[k], axis=0, tiled=True)
    current = [lax.axis_size(axes[k]) for k in reversed(sequence)]
    blocks = blocks.reshape(*current, *shard.shape)
    turned = sorted(range(len(sequence)), key=lambda place: sequence[len(sequence) - 1 - place])
    return blocks.transpose(*turned, *range(len(sequence), blocks.ndim)).reshape(-1, *shard.shape)


def gathered_by_axis(shard, axes, sequence, dim):
    return in_order(gather_in_order(shard, axes, sequence), dim)


def layer_norm(entries, scale_gain):
    average = jnp.mean(entries, axis=-1, keepdims=True)
    centred = entries - average
    variance = jnp.mean(centred * centred, axis=-1, keepdims=True)
    return centred * lax.rsqrt(variance + EPS) * scale_gain


def score_gradient(difference):
    return difference * lax.rsqrt(difference * difference + SMOOTH * SMOOTH)


def times_rows(left_side, right_side):
    return lax.dot_general(
        left_side, right_side, (((1,), (1,)), ((), ())), preferred_element_type=jnp.float32
    )


def banded_attention(query_rows, bordered, first_query, first_key, node_total, reaches):
    query_count = query_rows.shape[0]
    key_count = bordered.shape[0]
    model_width = query_rows.shape[1]
    key_heads = bordered[:, :model_width].reshape(key_count, HEADS, HEAD_DIM)
    value_heads = bordered[:, model_width:].reshape(key_count, HEADS, HEAD_DIM)
    queries = query_rows.reshape(query_count, HEADS, HEAD_DIM)
    scores = jnp.einsum(
        "qhd,khd->hqk", queries, key_heads, preferred_element_type=jnp.float32
    ) * HEAD_DIM ** (-0.5)
    rows_at = first_query + jnp.arange(query_count, dtype=jnp.int32)
    cols_at = first_key + jnp.arange(key_count, dtype=jnp.int32)
    distance = jnp.abs(rows_at[:, None] - cols_at[None, :])
    allowed = (
        (distance <= reaches[:, None]) & (cols_at[None, :] >= 0) & (cols_at[None, :] < node_total)
    )
    masked = jnp.where(allowed[None], scores, -1e30)
    highest = jnp.max(masked, axis=-1, keepdims=True)
    weights = jnp.where(allowed[None], jnp.exp(masked - highest), 0.0)
    chances = (weights / jnp.sum(weights, axis=-1, keepdims=True)).astype(jnp.bfloat16)
    blended = jnp.einsum("hqk,khd->qhd", chances, value_heads, preferred_element_type=jnp.float32)
    return blended.reshape(query_count, model_width).astype(jnp.bfloat16)


def per_device(
    gridpoint_state,
    grid_truth,
    encoder_slots,
    encoder_count,
    node_reach,
    decoder_slots,
    member_perturb,
    embed_weight,
    norm_gains,
    qkv_weight,
    out_weight,
    up_weight,
    down_weight,
    head_weight,
):
    region = lax.axis_index(NODE)
    region_count = lax.axis_size(NODE)
    ensemble_size = lax.axis_size("member")
    member_index = lax.axis_index("member")
    grid_dev = gridpoint_state.shape[1]
    node_dev = encoder_slots.shape[0]
    model_width = embed_weight.shape[1]
    node_total = node_dev * region_count
    widened = with_halo(gridpoint_state, ((NODE, 1),), grid_dev)
    local_slots = encoder_slots - (region - 1) * grid_dev
    window = jnp.arange(3 * grid_dev, dtype=jnp.int32)
    tallies = jnp.zeros((node_dev, 3 * grid_dev), jnp.float32)
    for position in range(encoder_slots.shape[1]):
        live = position < encoder_count
        hits = (local_slots[:, position][:, None] == window[None, :]) & live[:, None]
        tallies = tallies + hits.astype(jnp.float32)
    pooled_sum = times_rows(tallies.astype(jnp.bfloat16), widened)
    pooled_nodes = (pooled_sum / encoder_count[:, None].astype(jnp.float32)).astype(jnp.bfloat16)
    embedded = jnp.dot(pooled_nodes, embed_weight, preferred_element_type=jnp.float32)
    hidden_start = embedded + member_perturb[0].astype(jnp.float32)
    normed = layer_norm(hidden_start, norm_gains[0]).astype(jnp.bfloat16)
    project = jnp.dot(normed, qkv_weight, preferred_element_type=jnp.float32).astype(jnp.bfloat16)
    query_rows = project[:, :model_width]
    bordered = with_halo(project[:, model_width:], ((NODE, 0),), BAND)
    first_query = region * node_dev
    attended = banded_attention(
        query_rows, bordered, first_query, first_query - BAND, node_total, node_reach
    )
    hidden_mid = hidden_start + jnp.dot(attended, out_weight, preferred_element_type=jnp.float32)
    normed_mid = layer_norm(hidden_mid, norm_gains[1]).astype(jnp.bfloat16)
    up_whole = gathered_by_axis(up_weight, NODE, (0, 1, 2), 0)
    upper = jnp.dot(normed_mid, up_whole, preferred_element_type=jnp.float32)
    active = jax.nn.gelu(upper).astype(jnp.bfloat16)
    down_whole = gathered_by_axis(down_weight, NODE, (0, 1, 2), 0)
    lowered = times_rows(active, down_whole)
    final = layer_norm(hidden_mid + lowered, norm_gains[2]).astype(jnp.bfloat16)
    local_nodes = decoder_slots - (region - 1) * node_dev
    variable_count = head_weight.shape[1]
    slot_count = decoder_slots.shape[1]
    projected = lax.dot_general(
        head_weight, final, (((0,), (1,)), ((), ())), preferred_element_type=jnp.float32
    )
    projected_near = with_halo(projected.astype(jnp.bfloat16), ((NODE, 1),), node_dev).astype(
        projected.dtype
    )
    summed = jnp.zeros((variable_count, grid_dev), jnp.float32)
    for position in range(slot_count):
        summed = summed + jnp.take(projected_near, local_nodes[:, position], axis=1)
    state_delta = summed / slot_count
    predicted_field = gridpoint_state[:variable_count].astype(jnp.float32) + state_delta
    pairwise_scale = 1.0 / (ensemble_size * (ensemble_size - 1))
    share = grid_dev // ensemble_size
    mine = lax.all_to_all(predicted_field[None], "member", split_axis=2, concat_axis=0, tiled=True)
    observed_field = lax.dynamic_slice_in_dim(grid_truth, member_index * share, share, 1).astype(
        jnp.float32
    )
    pairwise_sum = jnp.zeros_like(mine)
    for other_member in range(ensemble_size):
        pairwise_sum = pairwise_sum + score_gradient(mine - mine[other_member][None])
    gradients = (
        score_gradient(mine - observed_field[None]) / ensemble_size - pairwise_sum * pairwise_scale
    )
    return lax.all_to_all(
        gradients.astype(jnp.bfloat16), "member", split_axis=0, concat_axis=2, tiled=True
    ).astype(gradients.dtype)


def solution(mesh):
    torus = Mesh(
        mesh.devices.reshape(mesh.shape["member"], 2, 4, 8),
        ("member", "node_0", "node_1", "node_2"),
    )
    return jax.shard_map(
        per_device,
        mesh=torus,
        in_specs=(
            P(None, NODE),
            P(None, NODE),
            P(NODE, None),
            P(NODE),
            P(NODE),
            P(NODE, None),
            P("member", NODE, None),
            P(),
            P(),
            P(),
            P(),
            P(NODE, None),
            P(NODE, None),
            P(),
        ),
        out_specs=P("member", None, NODE),
        check_vma=False,
    )
```

profile of v0, /device:TPU:8, one launch (start us, length us, event | category | flops | bytes accessed | tf_op | source)
XLA Modules:
  0.0 375.4 jit_solution(6813843629020049477)
XLA Ops:
  6.6 7.8 %all-gather.1 = bf16[32,4096]{1,0:T(8,128)(2,1)} all-gather(bf16[16,4096]{1,0:T(8,128)(2,1)} %param.28), channel_id=3, replica_groups=mesh['member'=4,'node_0'=2,'node_1'=4,'node_2'=8] {'node_0'}, dimensions={0}, use_global_device_ids=true | all-gather | bytes 393216 | tf_op jit(solution)/shard_map/all_gather | solution.py:37
  14.5 6.0 %all-gather = bf16[32,4096]{1,0:T(8,128)(2,1)} all-gather(bf16[16,4096]{1,0:T(8,128)(2,1)} %param.27), channel_id=2, replica_groups=mesh['member'=4,'node_0'=2,'node_1'=4,'node_2'=8] {'node_0'}, dimensions={0}, use_global_device_ids=true | all-gather | bytes 393216 | tf_op jit(solution)/shard_map/all_gather | solution.py:37
  20.5 23.1 %all-gather.11.cloned.1.call-done = bf16[8,16,4096]{2,1,0:T(8,128)(2,1)} async-done(((bf16[2,16,4096]{2,1,0:T(8,128)(2,1)}), bf16[8,16,4096]{2,1,0:T(8,128)(2,1)}) %all-gather.11.cloned.1.call-update) | async-done | bytes 1048592 | tf_op jit(solution)/shard_map/all_gather | solution.py:37
  43.7 28.6 %all-gather.7.cloned.1.call-done = bf16[8,16,4096]{2,1,0:T(8,128)(2,1)} async-done(((bf16[2,16,4096]{2,1,0:T(8,128)(2,1)}), bf16[8,16,4096]{2,1,0:T(8,128)(2,1)}) %all-gather.7.cloned.1.call-update) | async-done | bytes 1048592 | tf_op jit(solution)/shard_map/all_gather | solution.py:37
  72.3 6.4 %collective-permute-start.1 = (bf16[218,1024]{1,0:T(8,128)(2,1)S(1)}, bf16[218,1024]{1,0:T(8,128)(2,1)S(1)}, u32[]{:S(2)}, u32[]{:S(2)}) collective-permute-start(bf16[218,1024]{1,0:T(8,128)(2,1)S(1)} %copy-done.4), channel_id=1, source_target_pairs={{1,0},{2,1},{3,2},{4,3},{5,4},{6,5},{7,6},{8,7},{9,8},{10,9},{11,1... | collective-permute-start | bytes 1339400 | tf_op jit(solution)/shard_map/ppermute | solution.py:23
  80.9 9.8 %collective-permute-done.1 = bf16[218,1024]{1,0:T(8,128)(2,1)S(1)} collective-permute-done((bf16[218,1024]{1,0:T(8,128)(2,1)S(1)}, bf16[218,1024]{1,0:T(8,128)(2,1)S(1)}, u32[]{:S(2)}, u32[]{:S(2)}) %collective-permute-start.1) | collective-permute-done | bytes 446496 | tf_op jit(solution)/shard_map/ppermute | solution.py:23
  90.7 11.8 %collective-permute-done = bf16[218,1024]{1,0:T(8,128)(2,1)} collective-permute-done((bf16[218,1024]{1,0:T(8,128)(2,1)S(1)}, bf16[218,1024]{1,0:T(8,128)(2,1)}, u32[]{:S(2)}, u32[]{:S(2)}) %collective-permute-start) | collective-permute-done | bytes 446496 | tf_op jit(solution)/shard_map/ppermute | solution.py:20
  102.5 12.2 %fusion.125 = (f32[256]{0:T(256)S(1)}, f32[256,1024]{1,0:T(8,128)S(1)}) fusion(bf16[1,256,1024]{2,1,0:T(8,128)(2,1)} %param.22, bf16[218,1024]{1,0:T(8,128)(2,1)} %param.23, bf16[218,1024]{1,0:T(8,128)(2,1)} %copy-done.12, bf16[218,1024]{1,0:T(8,128)(2,1)} %param.16, bf16[218,1024]{1,0:T(8,128)(2,1)} %collective-permute-done, s32[256]{0:T(256)S(1)} %bitcast.132, ...), kind=kOutput, calls=%fused_computation.198 | convolution fusion | flops 512426752 | bytes 3381248 | tf_op jit(solution)/shard_map/dot_general | solution.py:123
  115.0 5.0 %convolution_convert_fusion = bf16[256,3072]{1,0:T(8,128)(2,1)S(1)} fusion(bf16[1024,3072]{1,0:T(8,128)(2,1)} %param.25, f32[256,1024]{1,0:T(8,128)S(1)} %get-tuple-element.52, f32[1024]{0:T(1024)S(1)} %bitcast.130, f32[256]{0:T(256)S(1)} %add_rsqrt_fusion.2, f32[256]{0:T(256)S(1)} %broadcast_multiply_fusion.2), kind=kOutput, calls=%fused_computation.22 | convolution fusion | flops 1612447744 | bytes 8919040 | tf_op jit(solution)/shard_map/dot_general | solution.py:126
  123.0 3.9 %collective-permute-start.2 = (bf16[256,2048]{1,0:T(8,128)(2,1)}, bf16[256,2048]{1,0:T(8,128)(2,1)}, u32[]{:S(2)}, u32[]{:S(2)}) collective-permute-start(bf16[256,2048]{1,0:T(8,128)(2,1)} %slice.157), channel_id=1, source_target_pairs={{0,1},{1,2},{2,3},{3,4},{4,5},{5,6},{6,7},{7,8},{8,9},{9,10},{10,1... | collective-permute-start | bytes 3145736 | tf_op jit(solution)/shard_map/ppermute | solution.py:20
  129.3 2.0 copy.61
  131.4 37.4 %collective-permute-done.3 = bf16[256,2048]{1,0:T(8,128)(2,1)} collective-permute-done((bf16[256,2048]{1,0:T(8,128)(2,1)}, bf16[256,2048]{1,0:T(8,128)(2,1)}, u32[]{:S(2)}, u32[]{:S(2)}) %collective-permute-start.3) | collective-permute-done | bytes 1048608 | tf_op jit(solution)/shard_map/ppermute | solution.py:23
  168.8 6.1 %collective-permute-done.2 = bf16[256,2048]{1,0:T(8,128)(2,1)} collective-permute-done((bf16[256,2048]{1,0:T(8,128)(2,1)}, bf16[256,2048]{1,0:T(8,128)(2,1)}, u32[]{:S(2)}, u32[]{:S(2)}) %collective-permute-start.2) | collective-permute-done | bytes 1048608 | tf_op jit(solution)/shard_map/ppermute | solution.py:20
  174.9 2.1 pad_maximum_fusion
  179.0 2.6 copy.60
  181.6 2.6 copy.62
  184.2 11.4 %fusion.128 = (f32[16,256]{1,0:T(8,128)S(1)}, f32[16,256,768]{2,1,0:T(8,128)}) fusion(pred[256,768]{1,0:T(8,128)(4,1)S(1)} %fusion.90, bf16[256,16,64]{0,2,1:T(8,128)(2,1)} %bitcast.119, bf16[768,16,64]{0,2,1:T(8,128)(2,1)} %bitcast.115), kind=kOutput, calls=%fused_computation.199 | convolution fusion | flops 418382592 | bytes 14893056 | tf_op jit(solution)/shard_map/sub | solution.py:83
  195.6 7.1 %fusion.77 = bf16[16,64,256]{2,1,0:T(8,128)(2,1)S(1)} fusion(bf16[768,16,64]{0,2,1:T(8,128)(2,1)} %bitcast.114, f32[16,256,768]{2,1,0:T(8,128)} %get-tuple-element.54, f32[16,256]{1,0:T(8,128)S(1)} %get-tuple-element.53), kind=kOutput, calls=%fused_computation.103 | convolution fusion | flops 409206784 | bytes 14696448 | tf_op jit(solution)/shard_map/hqk,khd->qhd/dot_general | solution.py:85
  204.9 7.7 %copy.64 = bf16[2,4,8,16,4096]{4,3,2,1,0:T(8,128)(2,1)} copy(bf16[2,4,8,16,4096]{4,3,0,1,2:T(8,128)(2,1)} %bitcast.107) | data formatting | bytes 16777216 | tf_op jit(solution)/shard_map/transpose | solution.py:41
  212.6 74.4 %all-gather.9.cloned.1.call-done = bf16[64,16,4096]{2,1,0:T(8,128)(2,1)} async-done(((bf16[8,16,4096]{2,1,0:T(8,128)(2,1)}), bf16[64,16,4096]{2,1,0:T(8,128)(2,1)}) %all-gather.9.cloned.1.call-update) | async-done | bytes 8388624 | tf_op jit(solution)/shard_map/all_gather | solution.py:37
  287.0 7.8 %copy.63 = bf16[2,4,8,16,4096]{4,3,2,1,0:T(8,128)(2,1)} copy(bf16[2,4,8,16,4096]{4,3,0,1,2:T(8,128)(2,1)} %bitcast.108) | data formatting | bytes 16777216 | tf_op jit(solution)/shard_map/transpose | solution.py:41
  294.8 12.0 %fusion.130 = (f32[256]{0:T(256)S(1)}, f32[256,1024]{1,0:T(8,128)}) fusion(f32[256,1024]{1,0:T(8,128)S(1)} %copy-done.2, bf16[1024,4096]{1,0:T(8,128)(2,1)} %bitcast.109, bf16[1024,4096]{1,0:T(8,128)(2,1)} %bitcast.110, f32[1024]{0:T(1024)S(1)} %bitcast.129, f32[256]{0:T(256)S(1)} %add_rsqrt_fusion.1, f32[256]{0:T(256)S(1)} %broadcast_multiply_fusion.1), kind=kOutput, calls=%fused_computation.201 | convolution fusion | flops 4305977344 | bytes 18881536 | tf_op jit(solution)/shard_map/dot_general | solution.py:60
  309.9 5.4 %collective-permute-start.5 = (bf16[100,256]{1,0:T(8,128)(2,1)S(1)}, bf16[100,256]{1,0:T(8,128)(2,1)S(1)}, u32[]{:S(2)}, u32[]{:S(2)}) collective-permute-start(bf16[100,256]{1,0:T(8,128)(2,1)S(1)} %fusion.80), channel_id=1, source_target_pairs={{1,0},{2,1},{3,2},{4,3},{5,4},{6,5},{7,6},{8,7},{9,8},{10,9},{11,1... | collective-permute-start | bytes 153608 | tf_op jit(solution)/shard_map/ppermute | solution.py:23
  319.1 6.5 %collective-permute-done.4 = bf16[100,256]{1,0:T(8,128)(2,1)S(1)} collective-permute-done((bf16[100,256]{1,0:T(8,128)(2,1)S(1)}, bf16[100,256]{1,0:T(8,128)(2,1)S(1)}, u32[]{:S(2)}, u32[]{:S(2)}) %collective-permute-start.4) | collective-permute-done | bytes 51232 | tf_op jit(solution)/shard_map/ppermute | solution.py:20
  325.8 2.8 gather_fusion.3
  328.6 2.8 gather_fusion.2
  331.4 4.0 %gather_fusion.1 = f32[1024,100]{1,0:T(8,128)} fusion(f32[100,768]{0,1:T(8,128)S(1)} %copy.65, s32[1024]{0:T(1024)S(1)} %fusion.110), kind=kCustom, calls=%fused_computation.1.clone | custom fusion | bytes 823296 | tf_op jit(solution)/shard_map/jit(_take)/gather | solution.py:152
  335.5 4.0 %gather_fusion = f32[1024,100]{1,0:T(8,128)} fusion(f32[100,768]{0,1:T(8,128)S(1)} %copy.65, s32[1024]{0:T(1024)S(1)} %fusion.109), kind=kCustom, calls=%fused_computation.clone | custom fusion | bytes 823296 | tf_op jit(solution)/shard_map/jit(_take)/gather | solution.py:152
  339.5 3.8 %fusion.93 = f32[100,1024]{0,1:T(8,128)} fusion(f32[1024,100]{1,0:T(8,128)S(1)} %gather_fusion.3, f32[1024,100]{1,0:T(8,128)S(1)} %gather_fusion.2, f32[1024,100]{1,0:T(8,128)} %gather_fusion.1, f32[1024,100]{1,0:T(8,128)} %gather_fusion, bf16[100,1024]{0,1:T(8,128)(2,1)} %copy.73, pred[1024]{0:T(1024)(128)(4,1)S(1)} %get-tuple-element.61, ...), kind=kLoop, calls=%fused_computation.121 | loop fusion | flops 1024000 | bytes 2256896 | tf_op jit(solution)/shard_map/add | solution.py:154
  343.3 3.7 all-to-all-start
  347.7 9.5 %all-to-all-done = f32[1,100,1024]{1,0,2:T(1,128)S(1)} async-done(((f32[1,100,1024]{1,0,2:T(1,128)}), f32[1,100,1024]{1,0,2:T(1,128)S(1)}, u32[]{:S(2)}, u32[]{:S(2)}) %all-to-all-start) | async-done | bytes 409632 | tf_op jit(solution)/shard_map/all_to_all | solution.py:157
  358.0 9.4 %all_to_all.27 = bf16[4,100,256]{2,1,0:T(8,128)(2,1)S(1)} all-to-all(bf16[4,100,256]{2,1,0:T(8,128)(2,1)S(1)} %subtract_convert_fusion), channel_id=1, replica_groups=mesh['member'=4,'node_0'=2,'node_1'=4,'node_2'=8] {'member'}, dimensions={0} | all-to-all | bytes 409600 | tf_op jit(solution)/shard_map/all_to_all | solution.py:167
  (81 shorter events, 22.0 us)
Async XLA Ops:
  6.5 196.2 %copy-start = (bf16[1024,1024]{1,0:T(8,128)(2,1)S(1)}, bf16[1024,1024]{1,0:T(8,128)(2,1)}, u32[]{:S(2)}) copy-start(bf16[1024,1024]{1,0:T(8,128)(2,1)} %param.26) | copy-start | bytes 6291460
  6.5 65.8 %copy-start.4 = (bf16[218,1024]{1,0:T(8,128)(2,1)S(1)}, bf16[218,1024]{1,0:T(8,128)(2,1)}, u32[]{:S(2)}) copy-start(bf16[218,1024]{1,0:T(8,128)(2,1)} %param.16) | copy-start | bytes 1339396
  6.5 74.2 %copy-start.10 = (s32[256]{0:T(256)S(1)}, s32[256]{0:T(256)}, u32[]{:S(2)}) copy-start(s32[256]{0:T(256)} %param.19) | copy-start | bytes 3076
  6.5 74.2 %copy-start.5 = (s32[1024,4]{0,1:T(4,128)S(1)}, s32[1024,4]{0,1:T(4,128)}, u32[]{:S(2)}) copy-start(s32[1024,4]{0,1:T(4,128)} %param.21) | copy-start | bytes 49156
  6.5 74.3 %copy-start.6 = (s32[256,16]{0,1:T(8,128)S(1)}, s32[256,16]{0,1:T(8,128)}, u32[]{:S(2)}) copy-start(s32[256,16]{0,1:T(8,128)} %param.18) | copy-start | bytes 49156
  6.5 74.3 %copy-start.7 = (f32[3,1024]{1,0:T(4,128)S(1)}, f32[3,1024]{1,0:T(4,128)}, u32[]{:S(2)}) copy-start(f32[3,1024]{1,0:T(4,128)} %param.24) | copy-start | bytes 36868
  6.6 37.0 %all-gather.11.cloned.1.call-start = ((), (), s32[]{:S(2)}) async-start(), calls=%async_computation.4 | async-start | bytes 1310720 | tf_op jit(solution)/shard_map/all_gather | solution.py:37
  14.4 57.9 %all-gather.7.cloned.1.call-start = ((), (), s32[]{:S(2)}) async-start(), calls=%async_computation.2 | async-start | bytes 1310720 | tf_op jit(solution)/shard_map/all_gather | solution.py:37
  20.5 184.4 %all-gather.13.cloned.1.call-start = ((), (), s32[]{:S(2)}) async-start(), calls=%async_computation.5 | async-start | bytes 9437184 | tf_op jit(solution)/shard_map/all_gather | solution.py:37
  43.6 243.4 %all-gather.9.cloned.1.call-start = ((), (), s32[]{:S(2)}) async-start(), calls=%async_computation.3 | async-start | bytes 9437184 | tf_op jit(solution)/shard_map/all_gather | solution.py:37
  72.3 18.4 %collective-permute-start.1 = (bf16[218,1024]{1,0:T(8,128)(2,1)S(1)}, bf16[218,1024]{1,0:T(8,128)(2,1)S(1)}, u32[]{:S(2)}, u32[]{:S(2)}) collective-permute-start(bf16[218,1024]{1,0:T(8,128)(2,1)S(1)} %copy-done.4), channel_id=1, source_target_pairs={{1,0},{2,1},{3,2},{4,3},{5,4},{6,5},{7,6},{8,7},{9,8},{10,9},{11,1... | collective-permute-start | bytes 1339400 | tf_op jit(solution)/shard_map/ppermute | solution.py:23
  78.8 23.8 %collective-permute-start = (bf16[218,1024]{1,0:T(8,128)(2,1)S(1)}, bf16[218,1024]{1,0:T(8,128)(2,1)}, u32[]{:S(2)}, u32[]{:S(2)}) collective-permute-start(bf16[218,1024]{1,0:T(8,128)(2,1)S(1)} %copy-done.4), channel_id=1, source_target_pairs={{0,1},{1,2},{2,3},{3,4},{4,5},{5,6},{6,7},{7,8},{8,9},{9,10},{10,1... | collective-permute-start | bytes 1339400 | tf_op jit(solution)/shard_map/ppermute | solution.py:20
  90.7 11.8 %copy-start.12 = (bf16[218,1024]{1,0:T(8,128)(2,1)}, bf16[218,1024]{1,0:T(8,128)(2,1)S(1)}, u32[]{:S(2)}) copy-start(bf16[218,1024]{1,0:T(8,128)(2,1)S(1)} %collective-permute-done.1) | copy-start | bytes 1339396
  115.0 13.2 %copy-start.11 = (s32[256]{0:T(256)S(1)}, s32[256]{0:T(256)}, u32[]{:S(2)}) copy-start(s32[256]{0:T(256)} %param.20) | copy-start | bytes 3076
  121.1 47.7 %collective-permute-start.3 = (bf16[256,2048]{1,0:T(8,128)(2,1)}, bf16[256,2048]{1,0:T(8,128)(2,1)}, u32[]{:S(2)}, u32[]{:S(2)}) collective-permute-start(bf16[256,2048]{1,0:T(8,128)(2,1)} %slice.157), channel_id=1, source_target_pairs={{1,0},{2,1},{3,2},{4,3},{5,4},{6,5},{7,6},{8,7},{9,8},{10,9},{11,1... | collective-permute-start | bytes 3145736 | tf_op jit(solution)/shard_map/ppermute | solution.py:23
  123.0 52.0 %collective-permute-start.2 = (bf16[256,2048]{1,0:T(8,128)(2,1)}, bf16[256,2048]{1,0:T(8,128)(2,1)}, u32[]{:S(2)}, u32[]{:S(2)}) collective-permute-start(bf16[256,2048]{1,0:T(8,128)(2,1)} %slice.157), channel_id=1, source_target_pairs={{0,1},{1,2},{2,3},{3,4},{4,5},{5,6},{6,7},{7,8},{8,9},{9,10},{10,1... | collective-permute-start | bytes 3145736 | tf_op jit(solution)/shard_map/ppermute | solution.py:20
  203.5 1.0 copy-start.1
  287.0 7.8 %copy-start.2 = (f32[256,1024]{1,0:T(8,128)S(1)}, f32[256,1024]{1,0:T(8,128)}, u32[]{:S(2)}) copy-start(f32[256,1024]{1,0:T(8,128)} %copy-done.1) | copy-start | bytes 3145732
  294.8 13.5 %copy-start.3 = (bf16[1024,100]{0,1:T(8,128)(2,1)S(1)}, bf16[1024,100]{0,1:T(8,128)(2,1)}, u32[]{:S(2)}) copy-start(bf16[1024,100]{0,1:T(8,128)(2,1)} %param.29) | copy-start | bytes 614404
  309.9 9.2 %collective-permute-start.5 = (bf16[100,256]{1,0:T(8,128)(2,1)S(1)}, bf16[100,256]{1,0:T(8,128)(2,1)S(1)}, u32[]{:S(2)}, u32[]{:S(2)}) collective-permute-start(bf16[100,256]{1,0:T(8,128)(2,1)S(1)} %fusion.80), channel_id=1, source_target_pairs={{1,0},{2,1},{3,2},{4,3},{5,4},{6,5},{7,6},{8,7},{9,8},{10,9},{11,1... | collective-permute-start | bytes 153608 | tf_op jit(solution)/shard_map/ppermute | solution.py:23
  315.3 10.2 %collective-permute-start.4 = (bf16[100,256]{1,0:T(8,128)(2,1)S(1)}, bf16[100,256]{1,0:T(8,128)(2,1)S(1)}, u32[]{:S(2)}, u32[]{:S(2)}) collective-permute-start(bf16[100,256]{1,0:T(8,128)(2,1)S(1)} %fusion.80), channel_id=1, source_target_pairs={{0,1},{1,2},{2,3},{3,4},{4,5},{5,6},{6,7},{7,8},{8,9},{9,10},{10,1... | collective-permute-start | bytes 153608 | tf_op jit(solution)/shard_map/ppermute | solution.py:20
  331.4 8.1 %copy-start.8 = (pred[1024]{0:T(1024)(128)(4,1)S(1)}, pred[1024]{0:T(1024)(128)(4,1)}, u32[]{:S(2)}) copy-start(pred[1024]{0:T(1024)(128)(4,1)} %get-tuple-element.62) | copy-start | bytes 3076
  335.5 4.0 %copy-start.9 = (pred[1024]{0:T(1024)(128)(4,1)S(1)}, pred[1024]{0:T(1024)(128)(4,1)}, u32[]{:S(2)}) copy-start(pred[1024]{0:T(1024)(128)(4,1)} %get-tuple-element.63) | copy-start | bytes 3076
  343.3 14.0 %all-to-all-start = ((f32[1,100,1024]{1,0,2:T(1,128)}), f32[1,100,1024]{1,0,2:T(1,128)S(1)}, u32[]{:S(2)}, u32[]{:S(2)}) async-start(f32[1,100,1024]{1,0,2:T(1,128)} %bitcast.113), calls=%async_computation | async-start | bytes 1048576 | tf_op jit(solution)/shard_map/all_to_all | solution.py:157
Sparse Core Ops, SparseCore 0:
  14.5 29.0 all-gather.10
  45.4 26.8 all-gather.6
  74.1 120.2 all-gather.12
  196.0 90.8 all-gather.8
where the time goes:
time: 376 us; the launch traced here: 375 us
  waiting for transfers between devices  207 us (55%)
  matrix products  50.1 us (13%)
  local copies, waits for them, and re-layouts  45.2 us (12%)
  starting transfers between devices  25.3 us (7%)
  blocking collectives  23.1 us (6%)
  between operations  13.5 us (4%)
  other arithmetic  10.8 us (3%)
    all_gather x4, waiting for transfers between devices, gather_in_order(): blocks = lax.all_gather(blocks, axes[k], axis=0, tiled=True)  126 us
    ppermute x3, waiting for transfers between devices, with_halo(): lax.ppermute(lax.slice_in_dim(block, 0, width, axis=dim), axis, backward)  47.2 us
    ppermute x3, waiting for transfers between devices, with_halo(): lax.ppermute(lax.slice_in_dim(block, block.shape[dim] - width, None, axis...  24.5 us
    transpose x2, local copies, waits for them, and re-layouts, gather_in_order(): blocks.transpose(*turned, *range(len(sequence), blocks.ndim))  15.6 us
    all_gather x2, blocking collectives, gather_in_order(): blocks = lax.all_gather(blocks, axes[k], axis=0, tiled=True)  13.8 us
    ppermute x3, starting transfers between devices, with_halo(): lax.ppermute(lax.slice_in_dim(block, 0, width, axis=dim), axis, backward)  13.7 us
    gather x4, local copies, waits for them, and re-layouts, per_device(): summed = summed + jnp.take(projected_near, local_nodes[:, position], axis=1)  13.7 us
    dot_general x1, matrix products, per_device(): jnp.dot(pooled_nodes, embed_weight, preferred_element_type=jnp.float32)  12.2 us
  transfers between devices with their start and end apart: 11, of which 9 were waited for; matrix products, arithmetic and copies ran while one was open for 17% of the time, Pallas kernels for 0%

commit v1 on v0

--- a/solution.py
+++ b/solution.py
@@ -34,7 +34,9 @@
 def gather_in_order(shard, axes, sequence):
     blocks = shard[None]
     for k in sequence:
-        blocks = lax.all_gather(blocks, axes[k], axis=0, tiled=True)
+        blocks = jnp.concatenate(
+            lax.all_to_all(jnp.stack([blocks] * lax.axis_size(axes[k])), axes[k], 0, 0), axis=0
+        )
     current = [lax.axis_size(axes[k]) for k in reversed(sequence)]
     blocks = blocks.reshape(*current, *shard.shape)
     turned = sorted(range(len(sequence)), key=lambda place: sequence[len(sequence) - 1 - place])

time: 376 us -> 606 us (1.61)
  blocking collectives: 23.1 us -> 238 us
  between operations: 13.5 us -> 0.45 us
  waiting for transfers between devices: 207 us -> 217 us
  starting transfers between devices: 25.3 us -> 35.2 us
    all_to_all x0 -> x4, blocking collectives: none -> 228 us  [gather_in_order(): lax.all_to_all(jnp.stack([blocks] * lax.axis_size(axes[k])), axes[k], 0, 0)]
    ppermute x3, waiting for transfers between devices: 47.2 us -> 192 us  [with_halo(): lax.ppermute(lax.slice_in_dim(block, 0, width, axis=dim), axis, backward)]
    all_gather x4 -> x0, waiting for transfers between devices: 126 us -> none  [gather_in_order(): blocks = lax.all_gather(blocks, axes[k], axis=0, tiled=True)]
    all_gather x2 -> x0, blocking collectives: 13.8 us -> none  [gather_in_order(): blocks = lax.all_gather(blocks, axes[k], axis=0, tiled=True)]
    all_to_all x0 -> x2, starting transfers between devices: none -> 10.8 us  [gather_in_order(): lax.all_to_all(jnp.stack([blocks] * lax.axis_size(axes[k])), axes[k], 0, 0)]
    ppermute x3, waiting for transfers between devices: 24.5 us -> 13.9 us  [with_halo(): lax.ppermute(lax.slice_in_dim(block, block.shape[dim] - width, None, axis...]
  transfers between devices with their start and end apart: 11 -> 9, of which waited for: 9 -> 7; matrix products, arithmetic and copies ran while one was open for 17% -> 10% of each run, Pallas kernels for 0% -> 0%
where the time goes in v1:
time: 606 us; the launch traced here: 605 us
  blocking collectives  238 us (39%)
  waiting for transfers between devices  217 us (36%)
  local copies, waits for them, and re-layouts  50.7 us (8%)
  matrix products  50 us (8%)
  starting transfers between devices  35.2 us (6%)
  other arithmetic  13.5 us (2%)
    all_to_all x4, blocking collectives, gather_in_order(): lax.all_to_all(jnp.stack([blocks] * lax.axis_size(axes[k])), axes[k], 0, 0)  228 us
    ppermute x3, waiting for transfers between devices, with_halo(): lax.ppermute(lax.slice_in_dim(block, 0, width, axis=dim), axis, backward)  192 us
    transpose x2, local copies, waits for them, and re-layouts, gather_in_order(): blocks.transpose(*turned, *range(len(sequence), blocks.ndim))  15.6 us
    ppermute x3, waiting for transfers between devices, with_halo(): lax.ppermute(lax.slice_in_dim(block, block.shape[dim] - width, None, axis...  13.9 us
    gather x4, local copies, waits for them, and re-layouts, per_device(): summed = summed + jnp.take(projected_near, local_nodes[:, position], axis=1)  13.7 us
    ppermute x3, starting transfers between devices, with_halo(): lax.ppermute(lax.slice_in_dim(block, 0, width, axis=dim), axis, backward)  12.7 us
    dot_general x1, matrix products, per_device(): jnp.dot(pooled_nodes, embed_weight, preferred_element_type=jnp.float32)  12.1 us
  transfers between devices with their start and end apart: 9, of which 7 were waited for; matrix products, arithmetic and copies ran while one was open for 10% of the time, Pallas kernels for 0%

profile of v1, /device:TPU:8, one launch (start us, length us, event | category | flops | bytes accessed | tf_op | source)
XLA Modules:
  0.0 605.1 jit_solution(11800743008855994962)
XLA Ops:
  1.8 5.6 all-to-all-start.3
  10.6 7.6 %all_to_all.57 = bf16[2,1,16,4096]{3,2,1,0:T(8,128)(2,1)S(1)} all-to-all(bf16[2,1,16,4096]{3,2,1,0:T(8,128)(2,1)S(1)} %pad_maximum_fusion.1), channel_id=1, replica_groups=mesh['member'=4,'node_0'=2,'node_1'=4,'node_2'=8] {'node_0'}, dimensions={0} | all-to-all | bytes 524288 | tf_op jit(solution)/shard_map/all_to_all | solution.py:38
  18.3 16.0 %all_to_all.58 = bf16[4,2,16,4096]{3,2,1,0:T(8,128)(2,1)S(1)} all-to-all(bf16[4,2,16,4096]{3,2,1,0:T(8,128)(2,1)S(1)} %stack.22), channel_id=1, replica_groups=mesh['member'=4,'node_0'=2,'node_1'=4,'node_2'=8] {'node_1'}, dimensions={0} | all-to-all | bytes 2097152 | tf_op jit(solution)/shard_map/all_to_all | solution.py:38
  34.4 14.6 %all_to_all.59 = bf16[4,2,16,4096]{3,2,1,0:T(8,128)(2,1)S(1)} all-to-all(bf16[4,2,16,4096]{3,2,1,0:T(8,128)(2,1)S(1)} %stack.19), channel_id=1, replica_groups=mesh['member'=4,'node_0'=2,'node_1'=4,'node_2'=8] {'node_1'}, dimensions={0} | all-to-all | bytes 2097152 | tf_op jit(solution)/shard_map/all_to_all | solution.py:38
  50.0 190.2 %all_to_all.60 = bf16[8,8,16,4096]{3,2,1,0:T(8,128)(2,1)} all-to-all(bf16[8,8,16,4096]{3,2,1,0:T(8,128)(2,1)S(1)} %stack.23), channel_id=1, replica_groups=mesh['member'=4,'node_0'=2,'node_1'=4,'node_2'=8] {'node_2'}, dimensions={0} | all-to-all | bytes 16777216 | tf_op jit(solution)/shard_map/all_to_all | solution.py:38
  240.2 4.4 stack.20
  244.6 5.2 all-to-all-start.2
  249.8 6.8 %collective-permute-start.1 = (bf16[218,1024]{1,0:T(8,128)(2,1)S(1)}, bf16[218,1024]{1,0:T(8,128)(2,1)S(1)}, u32[]{:S(2)}, u32[]{:S(2)}) collective-permute-start(bf16[218,1024]{1,0:T(8,128)(2,1)S(1)} %copy-done.4), channel_id=1, source_target_pairs={{1,0},{2,1},{3,2},{4,3},{5,4},{6,5},{7,6},{8,7},{9,8},{10,9},{11,1... | collective-permute-start | bytes 1339400 | tf_op jit(solution)/shard_map/ppermute | solution.py:23
  259.0 176.9 %collective-permute-done.1 = bf16[218,1024]{1,0:T(8,128)(2,1)S(1)} collective-permute-done((bf16[218,1024]{1,0:T(8,128)(2,1)S(1)}, bf16[218,1024]{1,0:T(8,128)(2,1)S(1)}, u32[]{:S(2)}, u32[]{:S(2)}) %collective-permute-start.1) | collective-permute-done | bytes 446496 | tf_op jit(solution)/shard_map/ppermute | solution.py:23
  435.8 3.3 collective-permute-done
  439.1 12.1 %fusion.125 = (f32[256]{0:T(256)S(1)}, f32[256,1024]{1,0:T(8,128)S(1)}) fusion(bf16[1,256,1024]{2,1,0:T(8,128)(2,1)} %param.22, bf16[218,1024]{1,0:T(8,128)(2,1)} %param.23, bf16[218,1024]{1,0:T(8,128)(2,1)} %copy-done.12, bf16[218,1024]{1,0:T(8,128)(2,1)} %param.16, bf16[218,1024]{1,0:T(8,128)(2,1)} %collective-permute-done, s32[256]{0:T(256)S(1)} %bitcast.139, ...), kind=kOutput, calls=%fused_computation.200 | convolution fusion | flops 512426752 | bytes 3381248 | tf_op jit(solution)/shard_map/dot_general | solution.py:125
  451.5 4.9 convolution_convert_fusion
  457.5 3.9 collective-permute-start.3
  467.8 15.0 %collective-permute-done.3 = bf16[256,2048]{1,0:T(8,128)(2,1)} collective-permute-done((bf16[256,2048]{1,0:T(8,128)(2,1)}, bf16[256,2048]{1,0:T(8,128)(2,1)}, u32[]{:S(2)}, u32[]{:S(2)}) %collective-permute-start.3) | collective-permute-done | bytes 1048608 | tf_op jit(solution)/shard_map/ppermute | solution.py:23
  482.8 6.1 %collective-permute-done.2 = bf16[256,2048]{1,0:T(8,128)(2,1)} collective-permute-done((bf16[256,2048]{1,0:T(8,128)(2,1)}, bf16[256,2048]{1,0:T(8,128)(2,1)}, u32[]{:S(2)}, u32[]{:S(2)}) %collective-permute-start.2) | collective-permute-done | bytes 1048608 | tf_op jit(solution)/shard_map/ppermute | solution.py:20
  492.9 2.6 copy.60
  495.5 2.6 copy.62
  498.1 11.4 %fusion.128 = (f32[16,256]{1,0:T(8,128)S(1)}, f32[16,256,768]{2,1,0:T(8,128)}) fusion(pred[256,768]{1,0:T(8,128)(4,1)S(1)} %fusion.90, bf16[256,16,64]{0,2,1:T(8,128)(2,1)} %bitcast.124, bf16[768,16,64]{0,2,1:T(8,128)(2,1)} %bitcast.120), kind=kOutput, calls=%fused_computation.201 | convolution fusion | flops 418382592 | bytes 14893056 | tf_op jit(solution)/shard_map/sub | solution.py:85
  509.5 7.1 %fusion.77 = bf16[16,64,256]{2,1,0:T(8,128)(2,1)S(1)} fusion(bf16[768,16,64]{0,2,1:T(8,128)(2,1)} %bitcast.119, f32[16,256,768]{2,1,0:T(8,128)} %get-tuple-element.54, f32[16,256]{1,0:T(8,128)S(1)} %get-tuple-element.53), kind=kOutput, calls=%fused_computation.103 | convolution fusion | flops 409206784 | bytes 14696448 | tf_op jit(solution)/shard_map/hqk,khd->qhd/dot_general | solution.py:87
  518.8 7.7 %copy.64 = bf16[2,4,8,16,4096]{4,3,2,1,0:T(8,128)(2,1)} copy(bf16[2,4,8,16,4096]{4,3,0,1,2:T(8,128)(2,1)} %bitcast.111) | data formatting | bytes 16777216 | tf_op jit(solution)/shard_map/transpose | solution.py:43
  526.5 7.9 %copy.63 = bf16[2,4,8,16,4096]{4,3,2,1,0:T(8,128)(2,1)} copy(bf16[2,4,8,16,4096]{4,3,0,1,2:T(8,128)(2,1)} %bitcast.29) | data formatting | bytes 16777216 | tf_op jit(solution)/shard_map/transpose | solution.py:43
  534.4 12.1 %fusion.130 = (f32[256]{0:T(256)S(1)}, f32[256,1024]{1,0:T(8,128)}) fusion(f32[256,1024]{1,0:T(8,128)S(1)} %copy-done.2, bf16[1024,4096]{1,0:T(8,128)(2,1)} %bitcast.112, bf16[1024,4096]{1,0:T(8,128)(2,1)} %bitcast.113, f32[1024]{0:T(1024)S(1)} %bitcast.136, f32[256]{0:T(256)S(1)} %add_rsqrt_fusion.1, f32[256]{0:T(256)S(1)} %broadcast_multiply_fusion.1), kind=kOutput, calls=%fused_computation.203 | convolution fusion | flops 4305977344 | bytes 18881536 | tf_op jit(solution)/shard_map/dot_general | solution.py:62
  551.5 3.9 collective-permute-start.4
  557.2 4.5 collective-permute-done.4
  561.9 2.8 gather_fusion.3
  564.7 2.8 gather_fusion.2
  567.6 4.0 gather_fusion.1
  571.6 4.0 gather_fusion
  575.6 3.8 fusion.93
  579.4 3.9 all-to-all-start.6
  584.1 9.5 %all-to-all-done.6 = f32[1,100,1024]{1,0,2:T(1,128)S(1)} async-done(((f32[1,100,1024]{1,0,2:T(1,128)}), f32[1,100,1024]{1,0,2:T(1,128)S(1)}, u32[]{:S(2)}, u32[]{:S(2)}) %all-to-all-start.6) | async-done | bytes 409632 | tf_op jit(solution)/shard_map/all_to_all | solution.py:159
  594.3 9.4 %all_to_all.61 = bf16[4,100,256]{2,1,0:T(8,128)(2,1)S(1)} all-to-all(bf16[4,100,256]{2,1,0:T(8,128)(2,1)S(1)} %subtract_convert_fusion), channel_id=1, replica_groups=mesh['member'=4,'node_0'=2,'node_1'=4,'node_2'=8] {'member'}, dimensions={0} | all-to-all | bytes 409600 | tf_op jit(solution)/shard_map/all_to_all | solution.py:169
  (81 shorter events, 32.2 us)
Async XLA Ops:
  0.0 516.6 %copy-start = (bf16[1024,1024]{1,0:T(8,128)(2,1)S(1)}, bf16[1024,1024]{1,0:T(8,128)(2,1)}, u32[]{:S(2)}) copy-start(bf16[1024,1024]{1,0:T(8,128)(2,1)} %param.26) | copy-start | bytes 6291460
  1.8 8.8 %all-to-all-start.3 = ((bf16[2,1,16,4096]{3,2,1,0:T(8,128)(2,1)}), bf16[2,1,16,4096]{3,2,1,0:T(8,128)(2,1)S(1)}, u32[]{:S(2)}, u32[]{:S(2)}) async-start(bf16[2,1,16,4096]{3,2,1,0:T(8,128)(2,1)} %pad_maximum_fusion.2), calls=%async_computation.3 | async-start | bytes 524288 | tf_op jit(solution)/shard_map/all_to_all | solution.py:38
  244.6 5.2 copy-start.4
  244.6 14.1 %copy-start.10 = (s32[256]{0:T(256)S(1)}, s32[256]{0:T(256)}, u32[]{:S(2)}) copy-start(s32[256]{0:T(256)} %param.19) | copy-start | bytes 3076
  244.6 14.2 %copy-start.5 = (s32[1024,4]{0,1:T(4,128)S(1)}, s32[1024,4]{0,1:T(4,128)}, u32[]{:S(2)}) copy-start(s32[1024,4]{0,1:T(4,128)} %param.21) | copy-start | bytes 49156
  244.6 14.3 %copy-start.6 = (s32[256,16]{0,1:T(8,128)S(1)}, s32[256,16]{0,1:T(8,128)}, u32[]{:S(2)}) copy-start(s32[256,16]{0,1:T(8,128)} %param.18) | copy-start | bytes 49156
  244.6 14.3 %copy-start.7 = (f32[3,1024]{1,0:T(4,128)S(1)}, f32[3,1024]{1,0:T(4,128)}, u32[]{:S(2)}) copy-start(f32[3,1024]{1,0:T(4,128)} %param.24) | copy-start | bytes 36868
  244.6 281.9 %all-to-all-start.2 = ((bf16[8,8,16,4096]{3,2,1,0:T(8,128)(2,1)}), bf16[8,8,16,4096]{3,2,1,0:T(8,128)(2,1)}, u32[]{:S(2)}, u32[]{:S(2)}) async-start(bf16[8,8,16,4096]{3,2,1,0:T(8,128)(2,1)} %stack.20), calls=%async_computation.2 | async-start | bytes 16777216 | tf_op jit(solution)/shard_map/all_to_all | solution.py:38
  249.8 186.0 %collective-permute-start.1 = (bf16[218,1024]{1,0:T(8,128)(2,1)S(1)}, bf16[218,1024]{1,0:T(8,128)(2,1)S(1)}, u32[]{:S(2)}, u32[]{:S(2)}) collective-permute-start(bf16[218,1024]{1,0:T(8,128)(2,1)S(1)} %copy-done.4), channel_id=1, source_target_pairs={{1,0},{2,1},{3,2},{4,3},{5,4},{6,5},{7,6},{8,7},{9,8},{10,9},{11,1... | collective-permute-start | bytes 1339400 | tf_op jit(solution)/shard_map/ppermute | solution.py:23
  256.6 182.5 %collective-permute-start = (bf16[218,1024]{1,0:T(8,128)(2,1)S(1)}, bf16[218,1024]{1,0:T(8,128)(2,1)}, u32[]{:S(2)}, u32[]{:S(2)}) collective-permute-start(bf16[218,1024]{1,0:T(8,128)(2,1)S(1)} %copy-done.4), channel_id=1, source_target_pairs={{0,1},{1,2},{2,3},{3,4},{4,5},{5,6},{6,7},{7,8},{8,9},{9,10},{10,1... | collective-permute-start | bytes 1339400 | tf_op jit(solution)/shard_map/ppermute | solution.py:20
  435.8 3.3 copy-start.12
  451.5 13.1 %copy-start.11 = (s32[256]{0:T(256)S(1)}, s32[256]{0:T(256)}, u32[]{:S(2)}) copy-start(s32[256]{0:T(256)} %param.20) | copy-start | bytes 3076
  457.5 25.3 %collective-permute-start.3 = (bf16[256,2048]{1,0:T(8,128)(2,1)}, bf16[256,2048]{1,0:T(8,128)(2,1)}, u32[]{:S(2)}, u32[]{:S(2)}) collective-permute-start(bf16[256,2048]{1,0:T(8,128)(2,1)} %slice.157), channel_id=1, source_target_pairs={{1,0},{2,1},{3,2},{4,3},{5,4},{6,5},{7,6},{8,7},{9,8},{10,9},{11,1... | collective-permute-start | bytes 3145736 | tf_op jit(solution)/shard_map/ppermute | solution.py:23
  461.5 27.5 %collective-permute-start.2 = (bf16[256,2048]{1,0:T(8,128)(2,1)}, bf16[256,2048]{1,0:T(8,128)(2,1)}, u32[]{:S(2)}, u32[]{:S(2)}) collective-permute-start(bf16[256,2048]{1,0:T(8,128)(2,1)} %slice.157), channel_id=1, source_target_pairs={{0,1},{1,2},{2,3},{3,4},{4,5},{5,6},{6,7},{7,8},{8,9},{9,10},{10,1... | collective-permute-start | bytes 3145736 | tf_op jit(solution)/shard_map/ppermute | solution.py:20
  517.5 1.1 copy-start.1
  526.5 7.9 %copy-start.2 = (f32[256,1024]{1,0:T(8,128)S(1)}, f32[256,1024]{1,0:T(8,128)}, u32[]{:S(2)}) copy-start(f32[256,1024]{1,0:T(8,128)} %copy-done.1) | copy-start | bytes 3145732
  534.4 13.6 %copy-start.3 = (bf16[1024,100]{0,1:T(8,128)(2,1)S(1)}, bf16[1024,100]{0,1:T(8,128)(2,1)}, u32[]{:S(2)}) copy-start(bf16[1024,100]{0,1:T(8,128)(2,1)} %param.29) | copy-start | bytes 614404
  549.5 7.7 %collective-permute-start.5 = (bf16[100,256]{1,0:T(8,128)(2,1)S(1)}, bf16[100,256]{1,0:T(8,128)(2,1)S(1)}, u32[]{:S(2)}, u32[]{:S(2)}) collective-permute-start(bf16[100,256]{1,0:T(8,128)(2,1)S(1)} %fusion.80), channel_id=1, source_target_pairs={{1,0},{2,1},{3,2},{4,3},{5,4},{6,5},{7,6},{8,7},{9,8},{10,9},{11,1... | collective-permute-start | bytes 153608 | tf_op jit(solution)/shard_map/ppermute | solution.py:23
  551.5 10.2 %collective-permute-start.4 = (bf16[100,256]{1,0:T(8,128)(2,1)S(1)}, bf16[100,256]{1,0:T(8,128)(2,1)S(1)}, u32[]{:S(2)}, u32[]{:S(2)}) collective-permute-start(bf16[100,256]{1,0:T(8,128)(2,1)S(1)} %fusion.80), channel_id=1, source_target_pairs={{0,1},{1,2},{2,3},{3,4},{4,5},{5,6},{6,7},{7,8},{8,9},{9,10},{10,1... | collective-permute-start | bytes 153608 | tf_op jit(solution)/shard_map/ppermute | solution.py:20
  567.6 8.0 %copy-start.8 = (pred[1024]{0:T(1024)(128)(4,1)S(1)}, pred[1024]{0:T(1024)(128)(4,1)}, u32[]{:S(2)}) copy-start(pred[1024]{0:T(1024)(128)(4,1)} %get-tuple-element.62) | copy-start | bytes 3076
  571.6 4.0 copy-start.9
  579.4 14.2 %all-to-all-start.6 = ((f32[1,100,1024]{1,0,2:T(1,128)}), f32[1,100,1024]{1,0,2:T(1,128)S(1)}, u32[]{:S(2)}, u32[]{:S(2)}) async-start(f32[1,100,1024]{1,0,2:T(1,128)} %bitcast.118), calls=%async_computation.6 | async-start | bytes 1048576 | tf_op jit(solution)/shard_map/all_to_all | solution.py:159
